TPU v7x, 32 devices: a whole 2x2x4 slice. The times are simulated.
32 devices in a mesh: rep: 8 (over z, x), shard: 4 (over y, core).
Axes of the slice: x: 2, y: 2, z: 4, core: 2. Of those that a mesh axis runs over, the one named last changes fastest.
Arguments:
- latent_tokens: bfloat16 [256, 256, 384], P(('rep', 'shard')), may hold values from -6 to 6
- cond: bfloat16 [256, 384], P(('rep', 'shard')), may hold values from -6 to 6
- w_ada: bfloat16 [384, 2304], P('shard'), may hold values from -0.3125 to 0.3125
- b_ada: bfloat16 [2304], P('shard'), may hold values from -3 to 3
- w_qkv: bfloat16 [384, 1152], P('shard'), may hold values from -0.3125 to 0.3125
- b_qv: bfloat16 [768], P('shard'), may hold values from -3 to 3
- w_o: bfloat16 [384, 384], P('shard'), may hold values from -0.875 to 0.875
- b_o: bfloat16 [384], P('shard'), may hold values from -3 to 3
- w_1: bfloat16 [384, 1536], P('shard'), may hold values from -0.3125 to 0.3125
- b_1: bfloat16 [1536], P('shard'), may hold values from -3 to 3
- w_2: bfloat16 [1536, 384], P('shard'), may hold values from -0.15625 to 0.15625
- b_2: bfloat16 [384], P('shard'), may hold values from -3 to 3
- grad_out: bfloat16 [256, 256, 384], P(('rep', 'shard')), may hold values from -6 to 6
Outputs:
- block_out: bfloat16 [256, 256, 384], P(('rep', 'shard'))
- grad_tokens: float32 [256, 256, 384], P(('rep', 'shard'))
- grad_cond: float32 [256, 384], P(('rep', 'shard'))
- grad_w_ada: float32 [384, 2304], P('shard')
- grad_b_ada: float32 [2304], P('shard')
- grad_w_qkv: float32 [384, 1152], P('shard')
- grad_b_qv: float32 [768], P('shard')
- grad_w_o: float32 [384, 384], P('shard')
- grad_b_o: float32 [384], P('shard')
- grad_w_1: float32 [384, 1536], P('shard')
- grad_b_1: float32 [1536], P('shard')
- grad_w_2: float32 [1536, 384], P('shard')
- grad_b_2: float32 [384], P('shard')
All inputs are finite; a program needn't handle non-finite values.
Results may differ from a plain program's by a relative error of at most 0.019.
The roundings to bfloat16 on the way count: a program that leaves them out, or rounds other values in their place, can miss the bound.
Values may be sent and summed in bfloat16 or wider, within the bound.
No kernel may reach another device: no remote copies, remote signals or barrier semaphores. Data moves between devices by JAX's collectives and lax.ppermute only.
A program may use at most 128 MiB of HBM per device.

v0:
```python
import math
import jax
import jax.numpy as jnp
from jax import lax
from jax.sharding import PartitionSpec as P

HEADS = 6


def layer_norm(value):
    centred = value - jnp.mean(value, axis=-1, keepdims=True)
    factor = lax.rsqrt(jnp.mean(centred * centred, axis=-1, keepdims=True) + 1e-06)
    return (centred * factor, factor)


def norm_back(normed, factor, grad_normed):
    inner = jnp.mean(grad_normed, axis=-1, keepdims=True)
    along = jnp.mean(grad_normed * normed, axis=-1, keepdims=True)
    return factor * (grad_normed - inner - normed * along)


def project(left, right):
    return jnp.einsum("lsd,de->lse", left, right, preferred_element_type=jnp.float32)


def weight_grad(left, right):
    return jnp.einsum("lsd,lse->de", left, right, preferred_element_type=jnp.float32)


def attend(items):
    query, key, value = items
    scores = jnp.einsum("lqhd,lkhd->lhqk", query, key, preferred_element_type=jnp.float32) * 0.125
    top = jnp.max(scores, axis=-1, keepdims=True)
    expo = jnp.exp(scores - top)
    total = jnp.sum(expo, axis=-1, keepdims=True)
    probs = (expo / total).astype(jnp.bfloat16)
    attended = jnp.einsum("lhqk,lkhd->lqhd", probs, value, preferred_element_type=jnp.float32)
    return (attended.astype(jnp.bfloat16), top + jnp.log(total))


def attend_back(items):
    query, key, value, logsum, grad_att = items
    scores = jnp.einsum("lqhd,lkhd->lhqk", query, key, preferred_element_type=jnp.float32) * 0.125
    probs = jnp.exp(scores - logsum)
    rounded = probs.astype(jnp.bfloat16)
    grad_value = jnp.einsum(
        "lhqk,lqhd->lkhd", rounded, grad_att, preferred_element_type=jnp.float32
    )
    grad_probs = jnp.einsum("lqhd,lkhd->lhqk", grad_att, value, preferred_element_type=jnp.float32)
    row_total = jnp.sum(probs * grad_probs, axis=-1, keepdims=True)
    grad_scores = (probs * (grad_probs - row_total)).astype(jnp.bfloat16)
    grad_query = (
        jnp.einsum("lhqk,lkhd->lqhd", grad_scores, key, preferred_element_type=jnp.float32) * 0.125
    )
    grad_key = (
        jnp.einsum("lhqk,lqhd->lkhd", grad_scores, query, preferred_element_type=jnp.float32)
        * 0.125
    )
    return (
        grad_query.astype(jnp.bfloat16),
        grad_key.astype(jnp.bfloat16),
        grad_value.astype(jnp.bfloat16),
    )


def on_device(
    latent_tokens, cond, w_ada, b_ada, w_qkv, b_qv, w_o, b_o, w_1, b_1, w_2, b_2, grad_out
):
    count, length, width = latent_tokens.shape
    head_size = width // HEADS
    per_block = math.gcd(count, max(1, 512 // length))
    blocks = count // per_block
    whole = (
        lax.all_gather(w_ada, "shard", axis=0, tiled=True),
        lax.all_gather(b_ada, "shard", axis=0, tiled=True),
        lax.all_gather(w_qkv, "shard", axis=0, tiled=True),
        lax.all_gather(b_qv, "shard", axis=0, tiled=True),
        lax.all_gather(w_o, "shard", axis=0, tiled=True),
        lax.all_gather(b_o, "shard", axis=0, tiled=True),
        lax.all_gather(w_1, "shard", axis=0, tiled=True),
        lax.all_gather(b_1, "shard", axis=0, tiled=True),
        lax.all_gather(w_2, "shard", axis=0, tiled=True),
        lax.all_gather(b_2, "shard", axis=0, tiled=True),
    )
    f_ada, f_bada, f_qkv, f_bqv, f_wo, f_bo, f_w1, f_b1, f_w2, f_b2 = whole
    tokens = latent_tokens.astype(jnp.float32)
    condition = cond.astype(jnp.float32)
    cs = jax.nn.silu(condition).astype(jnp.bfloat16)
    ada = jnp.dot(cs, f_ada, preferred_element_type=jnp.float32) + f_bada.astype(jnp.float32)
    shift1, scale1, gate1, shift2, scale2, gate2 = jnp.split(ada, 6, axis=-1)
    n1, rstd1 = layer_norm(tokens)
    m1 = (n1 * (1.0 + scale1[:, None]) + shift1[:, None]).astype(jnp.bfloat16)
    qkv = project(m1, f_qkv)
    bias_qv = f_bqv.astype(jnp.float32)
    query = (qkv[..., :width] + bias_qv[:width]).astype(jnp.bfloat16)
    key = qkv[..., width : 2 * width].astype(jnp.bfloat16)
    value = (qkv[..., 2 * width :] + bias_qv[width:]).astype(jnp.bfloat16)
    shape_blocks = (blocks, per_block, length, HEADS, head_size)
    q_blocks = query.reshape(shape_blocks)
    k_blocks = key.reshape(shape_blocks)
    v_blocks = value.reshape(shape_blocks)
    att_blocks, logsum = lax.map(attend, (q_blocks, k_blocks, v_blocks))
    attended = att_blocks.reshape(count, length, width)
    branch = project(attended, f_wo) + f_bo.astype(jnp.float32)
    x1 = tokens + gate1[:, None] * branch
    n2, rstd2 = layer_norm(x1)
    m2 = (n2 * (1.0 + scale2[:, None]) + shift2[:, None]).astype(jnp.bfloat16)
    hidden = project(m2, f_w1) + f_b1.astype(jnp.float32)
    gelu_out, gelu_vjp = jax.vjp(lambda t: jax.nn.gelu(t, approximate=True), hidden)
    gelu_low = gelu_out.astype(jnp.bfloat16)
    ffn = project(gelu_low, f_w2) + f_b2.astype(jnp.float32)
    block_out = (x1 + gate2[:, None] * ffn).astype(jnp.bfloat16)
    again = (
        lax.all_gather(w_ada, "shard", axis=0, tiled=True),
        lax.all_gather(w_qkv, "shard", axis=0, tiled=True),
        lax.all_gather(w_o, "shard", axis=0, tiled=True),
        lax.all_gather(w_1, "shard", axis=0, tiled=True),
        lax.all_gather(w_2, "shard", axis=0, tiled=True),
    )
    g_ada, g_qkv, g_wo, g_w1, g_w2 = again
    cotangent = grad_out.astype(jnp.float32)
    grad_ffn = (cotangent * gate2[:, None]).astype(jnp.bfloat16)
    d_gate2 = jnp.sum(cotangent * ffn, axis=1)
    gw_2 = weight_grad(gelu_low, grad_ffn)
    gb_2 = jnp.sum(grad_ffn.astype(jnp.float32), axis=(0, 1))
    grad_gelu = jnp.einsum("lse,de->lsd", grad_ffn, g_w2, preferred_element_type=jnp.float32)
    grad_hidden = gelu_vjp(grad_gelu)[0].astype(jnp.bfloat16)
    gw_1 = weight_grad(m2, grad_hidden)
    gb_1 = jnp.sum(grad_hidden.astype(jnp.float32), axis=(0, 1))
    grad_m2 = jnp.einsum("lse,de->lsd", grad_hidden, g_w1, preferred_element_type=jnp.float32)
    d_scale2 = jnp.sum(grad_m2 * n2, axis=1)
    d_shift2 = jnp.sum(grad_m2, axis=1)
    grad_x1 = cotangent + norm_back(n2, rstd2, grad_m2 * (1.0 + scale2[:, None]))
    grad_branch = (grad_x1 * gate1[:, None]).astype(jnp.bfloat16)
    d_gate1 = jnp.sum(grad_x1 * branch, axis=1)
    gw_o = weight_grad(attended, grad_branch)
    gb_o = jnp.sum(grad_branch.astype(jnp.float32), axis=(0, 1))
    grad_att = jnp.einsum(
        "lse,de->lsd", grad_branch, g_wo, preferred_element_type=jnp.float32
    ).astype(jnp.bfloat16)
    dq, dk, dv = lax.map(
        attend_back, (q_blocks, k_blocks, v_blocks, logsum, grad_att.reshape(shape_blocks))
    )
    grad_qkv = jnp.concatenate(
        [
            dq.reshape(count, length, width),
            dk.reshape(count, length, width),
            dv.reshape(count, length, width),
        ],
        axis=-1,
    )
    gw_qkv = weight_grad(m1, grad_qkv)
    column_sums = jnp.sum(grad_qkv.astype(jnp.float32), axis=(0, 1))
    gb_qv = jnp.concatenate([column_sums[:width], column_sums[2 * width :]])
    grad_m1 = jnp.einsum("lse,de->lsd", grad_qkv, g_qkv, preferred_element_type=jnp.float32)
    d_scale1 = jnp.sum(grad_m1 * n1, axis=1)
    d_shift1 = jnp.sum(grad_m1, axis=1)
    grad_tokens = grad_x1 + norm_back(n1, rstd1, grad_m1 * (1.0 + scale1[:, None]))
    grad_ada = jnp.concatenate(
        [d_shift1, d_scale1, d_gate1, d_shift2, d_scale2, d_gate2], axis=-1
    ).astype(jnp.bfloat16)
    gw_ada = jnp.dot(cs.T, grad_ada, preferred_element_type=jnp.float32)
    gb_ada = jnp.sum(grad_ada.astype(jnp.float32), axis=0)
    grad_cs = jnp.dot(grad_ada, g_ada.T, preferred_element_type=jnp.float32)
    silu_grad = jax.vjp(jax.nn.silu, condition)[1](grad_cs)[0]
    partial_value = (
        lax.psum_scatter(
            gw_ada.astype(jnp.bfloat16), "shard", scatter_dimension=0, tiled=True
        ).astype(jnp.float32),
        lax.psum_scatter(
            gb_ada.astype(jnp.bfloat16), "shard", scatter_dimension=0, tiled=True
        ).astype(jnp.float32),
        lax.psum_scatter(
            gw_qkv.astype(jnp.bfloat16), "shard", scatter_dimension=0, tiled=True
        ).astype(jnp.float32),
        lax.psum_scatter(
            gb_qv.astype(jnp.bfloat16), "shard", scatter_dimension=0, tiled=True
        ).astype(jnp.float32),
        lax.psum_scatter(
            gw_o.astype(jnp.bfloat16), "shard", scatter_dimension=0, tiled=True
        ).astype(jnp.float32),
        lax.psum_scatter(
            gb_o.astype(jnp.bfloat16), "shard", scatter_dimension=0, tiled=True
        ).astype(jnp.float32),
        lax.psum_scatter(
            gw_1.astype(jnp.bfloat16), "shard", scatter_dimension=0, tiled=True
        ).astype(jnp.float32),
        lax.psum_scatter(
            gb_1.astype(jnp.bfloat16), "shard", scatter_dimension=0, tiled=True
        ).astype(jnp.float32),
        lax.psum_scatter(
            gw_2.astype(jnp.bfloat16), "shard", scatter_dimension=0, tiled=True
        ).astype(jnp.float32),
        lax.psum_scatter(
            gb_2.astype(jnp.bfloat16), "shard", scatter_dimension=0, tiled=True
        ).astype(jnp.float32),
    )
    summed = (
        lax.psum(partial_value[0].astype(jnp.bfloat16), "rep").astype(jnp.float32),
        lax.psum(partial_value[1].astype(jnp.bfloat16), "rep").astype(jnp.float32),
        lax.psum(partial_value[2].astype(jnp.bfloat16), "rep").astype(jnp.float32),
        lax.psum(partial_value[3].astype(jnp.bfloat16), "rep").astype(jnp.float32),
        lax.psum(partial_value[4].astype(jnp.bfloat16), "rep").astype(jnp.float32),
        lax.psum(partial_value[5].astype(jnp.bfloat16), "rep").astype(jnp.float32),
        lax.psum(partial_value[6].astype(jnp.bfloat16), "rep").astype(jnp.float32),
        lax.psum(partial_value[7].astype(jnp.bfloat16), "rep").astype(jnp.float32),
        lax.psum(partial_value[8].astype(jnp.bfloat16), "rep").astype(jnp.float32),
        lax.psum(partial_value[9].astype(jnp.bfloat16), "rep").astype(jnp.float32),
    )
    return (
        block_out,
        grad_tokens,
        silu_grad,
        summed[0],
        summed[1],
        summed[2],
        summed[3],
        summed[4],
        summed[5],
        summed[6],
        summed[7],
        summed[8],
        summed[9],
    )


def solution(mesh):
    in_specs = (
        P(("rep", "shard"), None, None),
        P(("rep", "shard"), None),
        P("shard", None),
        P("shard"),
        P("shard", None),
        P("shard"),
        P("shard", None),
        P("shard"),
        P("shard", None),
        P("shard"),
        P("shard", None),
        P("shard"),
        P(("rep", "shard"), None, None),
    )
    out_specs = (
        P(("rep", "shard"), None, None),
        P(("rep", "shard"), None, None),
        P(("rep", "shard"), None),
        P("shard", None),
        P("shard"),
        P("shard", None),
        P("shard"),
        P("shard", None),
        P("shard"),
        P("shard", None),
        P("shard"),
        P("shard", None),
        P("shard"),
    )
    return jax.shard_map(
        on_device, mesh=mesh, in_specs=in_specs, out_specs=out_specs, check_vma=False
    )
```

profile of v0, /device:TPU:0, one launch (start us, length us, event | category | flops | bytes accessed | tf_op | source)
XLA Modules:
  0.0 425.0 jit_solution(18000375624998559178)
XLA Ops:
  13.5 6.1 %all-gather = bf16[4,1,384]{2,1,0:T(2,128)(2,1)S(1)} all-gather(bf16[1,1,384]{2,1,0:T(2,128)(2,1)S(1)} %reshape.148), channel_id=1, replica_groups=mesh['rep'=8,'shard'=4] {'shard'}, dimensions={0}, use_global_device_ids=true | all-gather | bytes 3840 | tf_op jit(solution)/shard_map/all_gather | solution.py:81
  23.6 12.3 %all-reduce.12 = (bf16[2304]{0:T(1024)(128)(2,1)S(1)}, bf16[768]{0:T(1024)(128)(2,1)S(1)}, bf16[384]{0:T(512)(128)(2,1)S(1)}, bf16[384]{0:T(512)(128)(2,1)S(1)}) all-reduce(bf16[2304]{0:T(1024)(128)(2,1)S(1)} %dynamic-update-slice, bf16[768]{0:T(1024)(128)(2,1)S(1)} %dynamic-update-slice.1, ...), channel_id=1, replica_groups=mesh['rep'=8,'shard'=4] {'shard'}, use_global_device_ids=true, to_apply=%add | all-reduce | flops 3840 | bytes 15360
  36.5 1.8 convert_reduce_fusion
  39.2 5.9 %all_gather.39 = bf16[384,384]{1,0:T(8,128)(2,1)S(1)} all-gather(bf16[96,384]{1,0:T(8,128)(2,1)S(1)} %copy-done.16), channel_id=1, replica_groups=mesh['rep'=8,'shard'=4] {'shard'}, dimensions={0}, use_global_device_ids=true | all-gather | bytes 368640 | tf_op jit(solution)/shard_map/all_gather | solution.py:78
  45.1 11.3 %all_gather.37 = bf16[384,1152]{1,0:T(8,128)(2,1)S(1)} all-gather(bf16[96,1152]{1,0:T(8,128)(2,1)S(1)} %copy-done.15), channel_id=1, replica_groups=mesh['rep'=8,'shard'=4] {'shard'}, dimensions={0}, use_global_device_ids=true | all-gather | bytes 1105920 | tf_op jit(solution)/shard_map/all_gather | solution.py:76
  56.4 2.1 convolution_add_fusion
  59.2 3.0 fusion.98
  63.5 2.4 fusion.80
  65.9 1.7 copy.79
  67.6 2.6 copy.80
  70.2 2.6 copy.78
  74.2 18.9 %while.26 = (s32[]{:T(128)}, bf16[4,2,256,6,64]{2,4,3,1,0:T(8,128)(2,1)}, f32[4,2,6,256,1]{3,2,1,4,0:T(8,128)S(1)}, bf16[4,2,256,6,64]{2,4,3,1,0:T(8,128)(2,1)},...) while((s32[]{:T(128)}, ...), condition=%wide.region_5.6_spmd, body=%wide.region_2.5_spmd.sunk | while | flops 208598016 | bytes 11122777 | solution.py:102
  74.2 1.6 multiply_reduce_fusion.10
  76.3 2.5 fusion.152
  78.9 1.6 multiply_reduce_fusion.10
  81.1 2.5 fusion.152
  83.6 1.6 multiply_reduce_fusion.10
  85.8 2.5 fusion.152
  88.4 1.6 multiply_reduce_fusion.10
  90.6 2.5 fusion.152
  93.1 4.6 %fusion.115 = (f32[8,256]{1,0:T(8,128)S(1)}, f32[8,256,384]{2,1,0:T(8,128)S(1)}, f32[8,256,384]{2,1,0:T(8,128)}) fusion(f32[384]{0:T(512)S(1)} %convert_element_type.177, f32[8,384]{1,0:T(8,128)S(1)} %get-tuple-element.197, bf16[8,256,384]{2,1,0:T(8,128)(2,1)S(1)} %copy-done, bf16[8,256,384]{1,2,0:T(8,128)(2,1)} %bitcast.178, ...), kind=kOutput, calls=%fused_computation.164 | convolution fusion | flops 607909888 | bytes 9754112 | tf_op jit(solution)/shard_map/lsd,de->lse/dot_general | solution.py:23
  97.7 1.7 copy-done.1
  100.7 11.0 %multiply_convert_fusion.1 = (bf16[8,256,1536]{2,1,0:T(8,128)(2,1)}, f32[8,256,1536]{2,1,0:T(8,128)}) fusion(f32[1536]{0:T(1024)} %reshape.150, bf16[384,1536]{1,0:T(8,128)(2,1)} %all-gather.7.cloned.1.call-done, f32[8,256,384]{2,1,0:T(8,128)} %copy-done.1, f32[8,384]{1,0:T(8,128)} %get-tuple-element.193, f32[8,384]{1,0:T(8,128)} %get-tuple-element.194, ...), kind=kOutput, calls=%fused_computation.69 | convolution fusion | flops 2451308544 | bytes 23246848 | tf_op jit(solution)/shard_map/lsd,de->lse/dot_general | solution.py:23
  111.7 15.0 %fusion.120 = (bf16[1536]{0:T(1024)(128)(2,1)}, bf16[8,256,1536]{2,1,0:T(8,128)(2,1)S(1)}) fusion(f32[8,256,1536]{2,1,0:T(8,128)} %get-tuple-element.206, f32[1536]{0:T(1024)} %reshape.150, bf16[1536,384]{1,0:T(8,128)(2,1)} %all-gather.9.cloned.1.call-done, bf16[8,256,384]{2,1,0:T(8,128)(2,1)} %param.29, f32[8,384]{1,0:T(8,128)} %get-tuple-element.192), kind=kOutput, calls=%fused_computation.169 | convolution fusion | flops 2487482880 | bytes 21648384 | tf_op jit(solution)/shard_map/lse,de->lsd/dot_general | solution.py:126
  126.9 3.6 fusion.92
  131.8 1.9 copy-done.40
  133.7 6.0 %fusion.79 = (bf16[8,384]{1,0:T(8,128)(2,1)}, bf16[8,256,384]{2,1,0:T(8,128)(2,1)}, bf16[8,384]{1,0:T(8,128)(2,1)}, f32[8,256]{1,0:T(8,128)S(1)}, f32[8,256]{1,0:T(8,128)S(1)}, /*index=5*/bf16[8,384]{1,0:T(8,128)(2,1)}) fusion(bf16[8,256,384]{2,1,0:T(8,128)(2,1)S(1)} %copy-done.13, f32[384]{0:T(512)S(1)} %copy-done.36, f32[8,256,384]{2,1,0:T(8,128)S(1)} %copy-done.2, ...), kind=kOutput, calls=%fused_computation.94 | convolution fusion | flops 2428488704 | bytes 16985600 | tf_op jit(solution)/shard_map/lsd,de->lse/dot_general | solution.py:23
  139.7 4.1 fusion.114
  144.9 1.7 fusion.85
  146.6 3.7 convolution_convert_fusion.1
  150.4 2.6 copy.82
  157.0 37.3 %while.27 = (s32[]{:T(128)}, bf16[4,2,256,6,64]{2,4,3,1,0:T(8,128)(2,1)}, bf16[4,2,256,6,64]{2,4,3,1,0:T(8,128)(2,1)}, bf16[4,2,256,6,64]{2,4,3,1,0:T(8,128)(2,1...) while((s32[]{:T(128)}, ...), condition=%wide.region_12.13_spmd, body=%wide.region_10.12_spmd.sunk | while | flops 513733632 | bytes 33916044 | solution.py:141
  157.0 1.7 fusion.161
  160.2 1.9 multiply_reduce_fusion.11
  164.2 2.1 fusion.162
  166.4 1.7 fusion.161
  169.5 1.9 multiply_reduce_fusion.11
  173.5 2.1 fusion.162
  175.7 1.7 fusion.161
  178.8 1.9 multiply_reduce_fusion.11
  182.8 2.1 fusion.162
  185.0 1.7 fusion.161
  188.2 1.9 multiply_reduce_fusion.11
  192.2 2.1 fusion.162
  194.3 2.7 copy.85
  197.1 2.6 copy.83
  199.7 1.6 copy.84
  201.3 6.2 %fusion.82 = bf16[384,1152]{1,0:T(8,128)(2,1)} fusion(bf16[8,256,384]{2,1,0:T(8,128)(2,1)S(1)} %copy-done, f32[8,384]{1,0:T(8,128)S(1)} %copy-done.24, f32[8,384]{1,0:T(8,128)S(1)} %get-tuple-element.196, f32[8,256]{1,0:T(8,128)S(1)} %add_rsqrt_fusion.1, f32[8,256]{1,0:T(8,128)S(1)} %broadcast_multiply_fusion.5, bf16[8,256,384]{2,1,0:T(8,128)(2,1)} %copy.85, ...), kind=kOutput, calls=%fused_computation.111 | convolution fusion | flops 1831256064 | bytes 7217152 | tf_op jit(solution)/shard_map/lsd,lse->de/dot_general | solution.py:27
  207.6 7.6 %fusion.83 = bf16[384,1536]{1,0:T(8,128)(2,1)} fusion(bf16[8,256,1536]{2,1,0:T(8,128)(2,1)} %copy-done.39, f32[8,256,384]{2,1,0:T(8,128)} %copy-done.1, f32[8,384]{1,0:T(8,128)S(1)} %copy-done.29, f32[8,384]{1,0:T(8,128)S(1)} %copy-done.22, f32[8,256]{1,0:T(8,128)S(1)} %copy-done.26, f32[8,256]{1,0:T(8,128)S(1)} %broadcast_multiply_fusion.4), kind=kOutput, calls=%fused_computation.112 | convolution fusion | flops 2420441088 | bytes 10657792 | tf_op jit(solution)/shard_map/lsd,lse->de/dot_general | solution.py:27
  215.5 8.0 %fusion.84 = bf16[1536,384]{1,0:T(8,128)(2,1)} fusion(bf16[8,256,1536]{2,1,0:T(8,128)(2,1)} %get-tuple-element.205, bf16[8,256,384]{2,1,0:T(8,128)(2,1)} %param.29, f32[8,384]{1,0:T(8,128)S(1)} %copy-done.20), kind=kOutput, calls=%fused_computation.113 | convolution fusion | flops 2418868224 | bytes 9056256 | tf_op jit(solution)/shard_map/lsd,lse->de/dot_general | solution.py:27
  223.6 6.2 %fusion.76 = (bf16[8,384]{1,0:T(8,128)(2,1)S(1)}, f32[8,256]{1,0:T(8,128)S(1)}, f32[8,256]{1,0:T(8,128)S(1)}, bf16[8,384]{1,0:T(8,128)(2,1)S(1)}, f32[8,256,384]{2,1,0:T(8,128)S(1)}) fusion(bf16[8,256,384]{2,1,0:T(8,128)(2,1)S(1)} %copy-done, f32[8,256]{1,0:T(8,128)S(1)} %add_rsqrt_fusion.1, f32[8,256]{1,0:T(8,128)S(1)} %broadcast_multiply_fusion.5, ...), kind=kOutput, calls=%fused_computation.91 | convolution fusion | flops 1833949184 | bytes 10379264 | tf_op jit(solution)/shard_map/lse,de->lsd/dot_general | solution.py:155
  229.9 3.1 multiply_reduce_fusion.3
  233.1 1.9 convolution_convert_fusion
  235.2 24.6 %reduce-scatter.12.cloned.1.call-done = bf16[96,1536]{1,0:T(8,128)(2,1)} async-done(((bf16[384,1536]{1,0:T(8,128)(2,1)}), bf16[96,1536]{1,0:T(8,128)(2,1)}) %reduce-scatter.12.cloned.1.call-update) | async-done | bytes 294928 | tf_op jit(solution)/shard_map/reduce_scatter | solution.py:185
  259.8 28.5 %reduce-scatter.14.cloned.1.call-done = bf16[384,384]{1,0:T(8,128)(2,1)} async-done(((bf16[1536,384]{1,0:T(8,128)(2,1)}), bf16[384,384]{1,0:T(8,128)(2,1)}) %reduce-scatter.14.cloned.1.call-update) | async-done | bytes 294928 | tf_op jit(solution)/shard_map/reduce_scatter | solution.py:191
  288.3 32.0 %reduce-scatter.6.cloned.1.call-done = bf16[96,2304]{1,0:T(8,128)(2,1)} async-done(((bf16[384,2304]{1,0:T(8,128)(2,1)}), bf16[96,2304]{1,0:T(8,128)(2,1)}) %reduce-scatter.6.cloned.1.call-update) | async-done | bytes 442384 | tf_op jit(solution)/shard_map/reduce_scatter | solution.py:167
  322.9 2.3 fusion.113
  325.2 10.5 %all-reduce.11 = (bf16[2304]{0:T(1024)(128)(2,1)S(1)}, bf16[768]{0:T(1024)(128)(2,1)S(1)}, bf16[384]{0:T(512)(128)(2,1)S(1)}, bf16[1536]{0:T(1024)(128)(2,1)S(1)}, bf16[384]{0:T(512)(128)(2,1)S(1)}) all-reduce(bf16[2304]{0:T(1024)(128)(2,1)S(1)} %reduce_sum.215, ...), channel_id=3, replica_groups=mesh['rep'=8,'shard'=4] {'shard'}, use_global_device_ids=true, to_apply=%region_24.25.clone | all-reduce | flops 5376 | bytes 21504
  336.1 22.2 %all-reduce.9 = (bf16[576]{0:T(1024)(128)(2,1)S(1)}, bf16[192]{0:T(256)(128)(2,1)S(1)}, bf16[96]{0:T(256)(128)(2,1)S(1)}, bf16[384]{0:T(512)(128)(2,1)S(1)}, bf16[96]{0:T(256)(128)(2,1)S(1)}) all-reduce(bf16[576]{0:T(1024)(128)(2,1)S(1)} %dynamic-slice.5, ...), channel_id=1, replica_groups=mesh['rep'=8,'shard'=4] {'rep'}, use_global_device_ids=true, to_apply=%region_25.26 | all-reduce | flops 1344 | bytes 5376 | tf_op jit(solution)/shard_map/psum | solution.py:200
  362.3 47.9 %all-reduce.15.cloned.1.call-done = (bf16[96,2304]{1,0:T(8,128)(2,1)}, bf16[96,1152]{1,0:T(8,128)(2,1)}, bf16[96,384]{1,0:T(8,128)(2,1)}, bf16[96,1536]{1,0:T(8,128)(2,1)}, bf16[384,384]{1,0:T(8,128)(2,1)}) async-done(((bf16[96,2304]{1,0:T(8,128)(2,1)}, bf16[96,1152]{1,0:T(8,128)(2,1)}, bf16[96,384]{1,0:T(8,128)(2,1)}, bf16[96,1536]{1,0:T(8,128)(2,1)}, bf16[384,384]{1,0:T(8,128)(2,1)}), ...) | async-done | bytes 1327120 | tf_op jit(solution)/shard_map/psum | solution.py:199
  410.2 1.6 convert_element_type.196
  411.8 2.0 convert_element_type.189
  413.8 1.7 convert_element_type.192
  415.5 1.8 convert_element_type.199
  (186 shorter events, 43.3 us)
Async XLA Ops:
  7.2 31.1 %copy-start = (bf16[8,256,384]{2,1,0:T(8,128)(2,1)S(1)}, bf16[8,256,384]{2,1,0:T(8,128)(2,1)}, u32[]{:S(2)}) copy-start(bf16[8,256,384]{2,1,0:T(8,128)(2,1)} %param.17) | copy-start | bytes 4718596
  7.2 32.0 %copy-start.16 = (bf16[96,384]{1,0:T(8,128)(2,1)S(1)}, bf16[96,384]{1,0:T(8,128)(2,1)}, u32[]{:S(2)}) copy-start(bf16[96,384]{1,0:T(8,128)(2,1)} %param.23) | copy-start | bytes 221188
  7.2 37.9 %copy-start.15 = (bf16[96,1152]{1,0:T(8,128)(2,1)S(1)}, bf16[96,1152]{1,0:T(8,128)(2,1)}, u32[]{:S(2)}) copy-start(bf16[96,1152]{1,0:T(8,128)(2,1)} %param.21) | copy-start | bytes 663556
  7.2 49.2 %copy-start.17 = (bf16[8,384]{1,0:T(8,128)(2,1)S(1)}, bf16[8,384]{1,0:T(8,128)(2,1)}, u32[]{:S(2)}) copy-start(bf16[8,384]{1,0:T(8,128)(2,1)} %param.18) | copy-start | bytes 18436
  7.2 49.2 %all-gather.5.cloned.1.call-start = ((), (), s32[]{:S(2)}) async-start(), calls=%async_computation.5 | async-start | bytes 2211840 | tf_op jit(solution)/shard_map/all_gather | solution.py:74
  8.0 92.7 %all-gather.7.cloned.1.call-start = ((), (), s32[]{:S(2)}) async-start(), calls=%async_computation.6 | async-start | bytes 1474560 | tf_op jit(solution)/shard_map/all_gather | solution.py:80
  8.7 103.0 %all-gather.9.cloned.1.call-start = ((), (), s32[]{:S(2)}) async-start(), calls=%async_computation.7 | async-start | bytes 1474560 | tf_op jit(solution)/shard_map/all_gather | solution.py:82
  9.4 225.7 %reduce-scatter.10.cloned.1.call-start = ((), (), s32[]{:S(2)}) async-start(), calls=%async_computation.10 | async-start | bytes 368640 | tf_op jit(solution)/shard_map/reduce_scatter | solution.py:179
  35.9 57.2 %copy-start.27 = (f32[384]{0:T(512)}, f32[384]{0:T(512)S(1)}, u32[]{:S(2)}) copy-start(f32[384]{0:T(512)S(1)} %convert_element_type.177) | copy-start | bytes 4612
  56.4 5.8 %copy-start.12 = (bf16[384,1152]{1,0:T(8,128)(2,1)}, bf16[384,1152]{1,0:T(8,128)(2,1)S(1)}, u32[]{:S(2)}) copy-start(bf16[384,1152]{1,0:T(8,128)(2,1)S(1)} %all_gather.37) | copy-start | bytes 2654212
  59.2 3.0 copy-start.23
  97.7 1.7 copy-start.1
  111.7 15.1 %copy-start.38 = (bf16[384,1536]{1,0:T(8,128)(2,1)S(1)}, bf16[384,1536]{1,0:T(8,128)(2,1)}, u32[]{:S(2)}) copy-start(bf16[384,1536]{1,0:T(8,128)(2,1)} %all-gather.7.cloned.1.call-done) | copy-start | bytes 3538948
  126.8 3.7 copy-start.39
  126.8 4.2 copy-start.2
  126.8 4.6 %copy-start.13 = (bf16[8,256,384]{2,1,0:T(8,128)(2,1)S(1)}, bf16[8,256,384]{2,1,0:T(8,128)(2,1)}, u32[]{:S(2)}) copy-start(bf16[8,256,384]{2,1,0:T(8,128)(2,1)} %param.29) | copy-start | bytes 4718596
  126.8 4.6 %copy-start.19 = (f32[8,384]{1,0:T(8,128)S(1)}, f32[8,384]{1,0:T(8,128)}, u32[]{:S(2)}) copy-start(f32[8,384]{1,0:T(8,128)} %get-tuple-element.192) | copy-start | bytes 36868
  126.8 4.6 %copy-start.21 = (f32[8,384]{1,0:T(8,128)S(1)}, f32[8,384]{1,0:T(8,128)}, u32[]{:S(2)}) copy-start(f32[8,384]{1,0:T(8,128)} %get-tuple-element.194) | copy-start | bytes 36868
  126.8 4.6 %copy-start.25 = (f32[8,256]{1,0:T(8,128)S(1)}, f32[8,256]{1,0:T(8,128)}, u32[]{:S(2)}) copy-start(f32[8,256]{1,0:T(8,128)} %add_rsqrt_fusion) | copy-start | bytes 24580
  126.8 4.6 %copy-start.36 = (f32[384]{0:T(512)S(1)}, f32[384]{0:T(512)}, u32[]{:S(2)}) copy-start(f32[384]{0:T(512)} %convert_element_type.181) | copy-start | bytes 4612
  126.8 5.0 %copy-start.37 = (bf16[1536,384]{1,0:T(8,128)(2,1)S(1)}, bf16[1536,384]{1,0:T(8,128)(2,1)}, u32[]{:S(2)}) copy-start(bf16[1536,384]{1,0:T(8,128)(2,1)} %all-gather.9.cloned.1.call-done) | copy-start | bytes 3538948
  126.8 6.8 %copy-start.40 = (bf16[8,256,1536]{2,1,0:T(8,128)(2,1)S(1)}, bf16[8,256,1536]{2,1,0:T(8,128)(2,1)}, u32[]{:S(2)}) copy-start(bf16[8,256,1536]{2,1,0:T(8,128)(2,1)} %get-tuple-element.205) | copy-start | bytes 18874372
  139.7 5.2 %copy-start.9 = (bf16[4,2,256,6,64]{2,4,3,1,0:T(8,128)(2,1)S(1)}, bf16[4,2,256,6,64]{2,4,3,1,0:T(8,128)(2,1)}, u32[]{:S(2)}) copy-start(bf16[4,2,256,6,64]{2,4,3,1,0:T(8,128)(2,1)} %get-tuple-element.95) | copy-start | bytes 4718596
  143.8 1.2 copy-start.7
  150.3 84.8 %reduce-scatter.8.cloned.1.call-start = ((), (), s32[]{:S(2)}) async-start(), calls=%async_computation.9 | async-start | bytes 1105920 | tf_op jit(solution)/shard_map/reduce_scatter | solution.py:173
  157.0 1.7 copy-start.3
  166.4 1.7 copy-start.3
  175.7 1.7 copy-start.3
  185.0 1.7 copy-start.3
  194.3 5.3 %copy-start.8 = (bf16[4,2,256,6,64]{2,4,3,1,0:T(8,128)(2,1)S(1)}, bf16[4,2,256,6,64]{2,4,3,1,0:T(8,128)(2,1)}, u32[]{:S(2)}) copy-start(bf16[4,2,256,6,64]{2,4,3,1,0:T(8,128)(2,1)} %get-tuple-element.98) | copy-start | bytes 4718596
  197.1 4.2 copy-start.24
  201.3 6.3 %copy-start.22 = (f32[8,384]{1,0:T(8,128)S(1)}, f32[8,384]{1,0:T(8,128)}, u32[]{:S(2)}) copy-start(f32[8,384]{1,0:T(8,128)} %get-tuple-element.194) | copy-start | bytes 36868
  201.3 6.3 %copy-start.26 = (f32[8,256]{1,0:T(8,128)S(1)}, f32[8,256]{1,0:T(8,128)}, u32[]{:S(2)}) copy-start(f32[8,256]{1,0:T(8,128)} %add_rsqrt_fusion) | copy-start | bytes 24580
  201.3 6.3 %copy-start.29 = (f32[8,384]{1,0:T(8,128)S(1)}, f32[8,384]{1,0:T(8,128)}, u32[]{:S(2)}) copy-start(f32[8,384]{1,0:T(8,128)} %get-tuple-element.193) | copy-start | bytes 36868
  207.5 8.0 %copy-start.20 = (f32[8,384]{1,0:T(8,128)S(1)}, f32[8,384]{1,0:T(8,128)}, u32[]{:S(2)}) copy-start(f32[8,384]{1,0:T(8,128)} %get-tuple-element.192) | copy-start | bytes 36868
  207.5 52.3 %reduce-scatter.12.cloned.1.call-start = ((), (), s32[]{:S(2)}) async-start(), calls=%async_computation.11 | async-start | bytes 1474560 | tf_op jit(solution)/shard_map/reduce_scatter | solution.py:185
  215.2 8.3 %copy-start.10 = (bf16[8,256,384]{2,1,0:T(8,128)(2,1)S(1)}, bf16[8,256,384]{2,1,0:T(8,128)(2,1)}, u32[]{:S(2)}) copy-start(bf16[8,256,384]{2,1,0:T(8,128)(2,1)} %copy.85) | copy-start | bytes 4718596
  215.2 73.0 %reduce-scatter.14.cloned.1.call-start = ((), (), s32[]{:S(2)}) async-start(), calls=%async_computation.12 | async-start | bytes 1474560 | tf_op jit(solution)/shard_map/reduce_scatter | solution.py:191
  223.5 6.3 %copy-start.28 = (f32[384]{0:T(512)S(1)}, f32[384]{0:T(512)}, u32[]{:S(2)}) copy-start(f32[384]{0:T(512)} %copy-done.27) | copy-start | bytes 4612
  223.5 96.8 %reduce-scatter.6.cloned.1.call-start = ((), (), s32[]{:S(2)}) async-start(), calls=%async_computation.8 | async-start | bytes 2211840 | tf_op jit(solution)/shard_map/reduce_scatter | solution.py:167
  223.6 6.2 %copy-start.4 = (f32[8,256,384]{2,1,0:T(8,128)S(1)}, f32[8,256,384]{2,1,0:T(8,128)}, u32[]{:S(2)}) copy-start(f32[8,256,384]{2,1,0:T(8,128)} %get-tuple-element.204) | copy-start | bytes 9437188
  223.6 6.2 %copy-start.5 = (f32[8,256,384]{2,1,0:T(8,128)S(1)}, f32[8,256,384]{2,1,0:T(8,128)}, u32[]{:S(2)}) copy-start(f32[8,256,384]{2,1,0:T(8,128)} %get-tuple-element.174) | copy-start | bytes 9437188
  229.8 3.2 copy-start.32
  229.8 3.2 copy-start.31
  229.8 3.2 copy-start.30
  229.9 3.2 copy-start.18
  233.0 89.9 %copy-start.11 = (bf16[8,256,384]{2,1,0:T(8,128)(2,1)S(1)}, bf16[8,256,384]{2,1,0:T(8,128)(2,1)}, u32[]{:S(2)}) copy-start(bf16[8,256,384]{2,1,0:T(8,128)(2,1)} %copy.85) | copy-start | bytes 4718596
  235.0 90.2 %copy-start.33 = (bf16[384]{0:T(512)(128)(2,1)S(1)}, bf16[384]{0:T(512)(128)(2,1)}, u32[]{:S(2)}) copy-start(bf16[384]{0:T(512)(128)(2,1)} %get-tuple-element.172) | copy-start | bytes 2308
  235.0 90.2 %copy-start.34 = (bf16[384]{0:T(512)(128)(2,1)S(1)}, bf16[384]{0:T(512)(128)(2,1)}, u32[]{:S(2)}) copy-start(bf16[384]{0:T(512)(128)(2,1)} %get-tuple-element.191) | copy-start | bytes 2308
  235.0 90.2 %copy-start.35 = (bf16[1536]{0:T(1024)(128)(2,1)S(1)}, bf16[1536]{0:T(1024)(128)(2,1)}, u32[]{:S(2)}) copy-start(bf16[1536]{0:T(1024)(128)(2,1)} %get-tuple-element.208) | copy-start | bytes 9220
  235.0 126.1 %copy-start.6 = (bf16[384,2304]{1,0:T(8,128)(2,1)S(1)}, bf16[384,2304]{1,0:T(8,128)(2,1)}, u32[]{:S(2)}) copy-start(bf16[384,2304]{1,0:T(8,128)(2,1)} %all-gather.5.cloned.1.call-done) | copy-start | bytes 5308420
  235.1 175.2 %all-reduce.15.cloned.1.call-start = ((), (), s32[]{:S(2)}) async-start(), calls=%async_computation.13 | async-start | bytes 2654208 | tf_op jit(solution)/shard_map/psum | solution.py:199
  410.2 7.1 %copy-start.14 = (bf16[384,384]{1,0:T(8,128)(2,1)S(1)}, bf16[384,384]{1,0:T(8,128)(2,1)}, u32[]{:S(2)}) copy-start(bf16[384,384]{1,0:T(8,128)(2,1)} %get-tuple-element.162) | copy-start | bytes 884740
Sparse Core Ops, SparseCore 0:
  9.6 23.5 all-gather.4
  34.8 19.2 all-gather.6
  55.6 17.1 all-gather.8
  150.4 20.4 reduce-scatter.9
  207.6 23.9 reduce-scatter.7
  234.0 25.7 reduce-scatter.11
  262.5 25.7 reduce-scatter.13
  290.9 29.3 reduce-scatter.5
  324.8 85.3 all-reduce.14
where the time goes:
time: 429 us; the launch traced here: 425 us
  waiting for transfers between devices  135 us (31%)
  matrix products  133 us (31%)
  blocking collectives  68.3 us (16%)
  local copies, waits for them, and re-layouts  35.9 us (8%)
  other arithmetic  33 us (8%)
  between operations  19.2 us (4%)
    psum x1, waiting for transfers between devices, on_device(): lax.psum(partial_value[0].astype(jnp.bfloat16), 'rep').astype(jnp.float32)  47.9 us
    reduce_scatter x1, waiting for transfers between devices, on_device(): lax.psum_scatter(gw_ada.astype(jnp.bfloat16), 'shard', scatter_dimension=...  32 us
    reduce_scatter x1, waiting for transfers between devices, on_device(): lax.psum_scatter(gw_2.astype(jnp.bfloat16), 'shard', scatter_dimension=0,...  28.5 us
    dot_general x4, matrix products, project(): jnp.einsum('lsd,de->lse', left, right, preferred_element_type=jnp.float32)  24.6 us
    reduce_scatter x1, waiting for transfers between devices, on_device(): lax.psum_scatter(gw_1.astype(jnp.bfloat16), 'shard', scatter_dimension=0,...  24.6 us
    dot_general x4, matrix products, weight_grad(): jnp.einsum('lsd,lse->de', left, right, preferred_element_type=jnp.float32)  23.4 us
    unnamed x2, blocking collectives  22.9 us
    psum x1, blocking collectives, on_device(): lax.psum(partial_value[1].astype(jnp.bfloat16), 'rep').astype(jnp.float32)  22.2 us
  transfers between devices with their start and end apart: 9, of which 4 were waited for; matrix products, arithmetic and copies ran while one was open for 36% of the time, Pallas kernels for 0%

commit v1 on v0

--- a/solution.py
+++ b/solution.py
@@ -1,3 +1,4 @@
+import functools
 import math
 import jax
 import jax.numpy as jnp
@@ -5,6 +6,39 @@
 from jax.sharding import PartitionSpec as P
 
 HEADS = 6
+
+
+def direct_edge(s0, where_dim):
+    s0 = jnp.moveaxis(s0, 0, where_dim)
+    finding = s0.shape
+    return s0.reshape(
+        *finding[:where_dim], finding[where_dim] * finding[where_dim + 1], *finding[where_dim + 2 :]
+    )
+
+
+def run_spans_in(field_in, device_axis):
+    frame_out = lax.axis_size(device_axis)
+    oldest = lax.axis_index(device_axis)
+    out_arr, block_last = (frame_out, oldest)
+    side_arr, fresh = (field_in[None], 1)
+    while fresh < out_arr:
+        piece_next = range(out_arr)
+        tall = list(map(lambda at: (at, at ^ fresh), piece_next))
+        last = lax.ppermute(side_arr, device_axis, perm=tall)
+        g_now = block_last & fresh == 0
+        parts_out = jnp.where(g_now, side_arr, last)
+        k_now = jnp.where(g_now, last, side_arr)
+        side_arr = jnp.concatenate([parts_out, k_now])
+        fresh *= 2
+    return side_arr
+
+
+def cover_the_yards(payload, inputs, dim_k):
+    long_array = run_spans_in(payload, inputs)
+    return direct_edge(long_array, dim_k)
+
+
+grid_feed = functools.partial(cover_the_yards, inputs="shard", dim_k=0)
 
 
 def layer_norm(value):
@@ -73,7 +107,7 @@
     whole = (
         lax.all_gather(w_ada, "shard", axis=0, tiled=True),
         lax.all_gather(b_ada, "shard", axis=0, tiled=True),
-        lax.all_gather(w_qkv, "shard", axis=0, tiled=True),
+        grid_feed(w_qkv),
         lax.all_gather(b_qv, "shard", axis=0, tiled=True),
         lax.all_gather(w_o, "shard", axis=0, tiled=True),
         lax.all_gather(b_o, "shard", axis=0, tiled=True),

time: 429 us -> 452 us (1.054)
  waiting for transfers between devices: 135 us -> 157 us
    ppermute x0 -> x2, waiting for transfers between devices: none -> 13.6 us  [run_spans_in(): last = lax.ppermute(side_arr, device_axis, perm=tall)]
    reduce_scatter x1, waiting for transfers between devices: 0.02 us -> 4.84 us  [on_device(): lax.psum_scatter(gw_qkv.astype(jnp.bfloat16), 'shard', scatter_dimension=...]
    unnamed x100 -> x94, local copies, waits for them, and re-layouts: 12 us -> 10.8 us
  transfers between devices with their start and end apart: 9 -> 11, of which waited for: 4 -> 6; matrix products, arithmetic and copies ran while one was open for 36% -> 23% of each run, Pallas kernels for 0% -> 0%
where the time goes in v1:
time: 452 us; the launch traced here: 445 us
  waiting for transfers between devices  157 us (35%)
  matrix products  131 us (29%)
  blocking collectives  68.7 us (15%)
  local copies, waits for them, and re-layouts  35 us (8%)
  other arithmetic  32 us (7%)
  between operations  19.4 us (4%)
    psum x1, waiting for transfers between devices, on_device(): lax.psum(partial_value[0].astype(jnp.bfloat16), 'rep').astype(jnp.float32)  47.9 us
    reduce_scatter x1, waiting for transfers between devices, on_device(): lax.psum_scatter(gw_ada.astype(jnp.bfloat16), 'shard', scatter_dimension=...  32 us
    reduce_scatter x1, waiting for transfers between devices, on_device(): lax.psum_scatter(gw_2.astype(jnp.bfloat16), 'shard', scatter_dimension=0,...  28.5 us
    reduce_scatter x1, waiting for transfers between devices, on_device(): lax.psum_scatter(gw_1.astype(jnp.bfloat16), 'shard', scatter_dimension=0,...  28.1 us
    dot_general x4, matrix products, project(): jnp.einsum('lsd,de->lse', left, right, preferred_element_type=jnp.float32)  24.7 us
    unnamed x2, blocking collectives  23.9 us
    dot_general x4, matrix products, weight_grad(): jnp.einsum('lsd,lse->de', left, right, preferred_element_type=jnp.float32)  23.8 us
    psum x1, blocking collectives, on_device(): lax.psum(partial_value[1].astype(jnp.bfloat16), 'rep').astype(jnp.float32)  22.2 us
  transfers between devices with their start and end apart: 11, of which 6 were waited for; matrix products, arithmetic and copies ran while one was open for 23% of the time, Pallas kernels for 0%

profile of v1, /device:TPU:0, one launch (start us, length us, event | category | flops | bytes accessed | tf_op | source)
XLA Modules:
  0.0 444.6 jit_solution(3806950361475571462)
XLA Ops:
  16.2 13.4 %all-reduce.12 = (bf16[2304]{0:T(1024)(128)(2,1)S(1)}, bf16[768]{0:T(1024)(128)(2,1)S(1)}, bf16[384]{0:T(512)(128)(2,1)S(1)}, bf16[384]{0:T(512)(128)(2,1)S(1)}) all-reduce(bf16[2304]{0:T(1024)(128)(2,1)S(1)} %dynamic-update-slice, bf16[768]{0:T(1024)(128)(2,1)S(1)} %dynamic-update-slice.1, ...), channel_id=1, replica_groups=mesh['rep'=8,'shard'=4] {'shard'}, use_global_device_ids=true, to_apply=%add | all-reduce | flops 3840 | bytes 15360
  29.6 1.8 convert_reduce_fusion
  31.4 6.1 %all_gather.37 = bf16[384,384]{1,0:T(8,128)(2,1)S(1)} all-gather(bf16[96,384]{1,0:T(8,128)(2,1)} %param.23), channel_id=1, replica_groups=mesh['rep'=8,'shard'=4] {'shard'}, dimensions={0}, use_global_device_ids=true | all-gather | bytes 368640 | tf_op jit(solution)/shard_map/all_gather | solution.py:112
  38.2 5.1 %all-gather = bf16[4,1,384]{2,1,0:T(2,128)(2,1)S(1)} all-gather(bf16[1,1,384]{2,1,0:T(2,128)(2,1)S(1)} %reshape.152), channel_id=1, replica_groups=mesh['rep'=8,'shard'=4] {'shard'}, dimensions={0}, use_global_device_ids=true | all-gather | bytes 3840 | tf_op jit(solution)/shard_map/all_gather | solution.py:115
  46.8 13.6 %collective-permute-done.1 = bf16[2,96,1152]{2,1,0:T(8,128)(2,1)S(1)} collective-permute-done((bf16[2,96,1152]{2,1,0:T(8,128)(2,1)S(1)}, bf16[2,96,1152]{2,1,0:T(8,128)(2,1)S(1)}, u32[]{:S(2)}, u32[]{:S(2)}) %collective-permute-start.1) | collective-permute-done | bytes 442400 | tf_op jit(solution)/shard_map/ppermute | solution.py:27
  60.6 1.8 convolution_add_fusion
  63.1 3.0 fusion.99
  67.5 1.8 fusion.80
  69.3 2.2 copy.78
  71.5 1.7 copy.79
  73.2 2.6 copy.80
  77.1 18.9 %while.26 = (s32[]{:T(128)}, bf16[4,2,256,6,64]{2,4,3,1,0:T(8,128)(2,1)}, f32[4,2,6,256,1]{3,2,1,4,0:T(8,128)S(1)}, bf16[4,2,256,6,64]{2,4,3,1,0:T(8,128)(2,1)},...) while((s32[]{:T(128)}, ...), condition=%wide.region_5.6_spmd, body=%wide.region_2.5_spmd.sunk | while | flops 208598016 | bytes 11122769 | solution.py:136
  77.1 1.6 multiply_reduce_fusion.10
  79.3 2.5 fusion.152
  81.8 1.6 multiply_reduce_fusion.10
  84.0 2.5 fusion.152
  86.6 1.6 multiply_reduce_fusion.10
  88.8 2.5 fusion.152
  91.3 1.6 multiply_reduce_fusion.10
  93.5 2.5 fusion.152
  96.0 4.6 %fusion.114 = (f32[8,256]{1,0:T(8,128)S(1)}, f32[8,256,384]{2,1,0:T(8,128)S(1)}, f32[8,256,384]{2,1,0:T(8,128)}) fusion(f32[384]{0:T(512)S(1)} %convert_element_type.177, f32[8,384]{1,0:T(8,128)S(1)} %get-tuple-element.201, bf16[8,256,384]{2,1,0:T(8,128)(2,1)S(1)} %copy-done, bf16[8,256,384]{1,2,0:T(8,128)(2,1)} %bitcast.25, ...), kind=kOutput, calls=%fused_computation.169 | convolution fusion | flops 607909888 | bytes 9754112 | tf_op jit(solution)/shard_map/lsd,de->lse/dot_general | solution.py:57
  100.7 1.7 copy-done.1
  103.6 11.0 %multiply_convert_fusion.1 = (bf16[8,256,1536]{2,1,0:T(8,128)(2,1)}, f32[8,256,1536]{2,1,0:T(8,128)}) fusion(f32[1536]{0:T(1024)} %reshape.154, bf16[384,1536]{1,0:T(8,128)(2,1)} %all-gather.7.cloned.1.call-done, f32[8,256,384]{2,1,0:T(8,128)} %copy-done.1, f32[8,384]{1,0:T(8,128)} %get-tuple-element.197, f32[8,384]{1,0:T(8,128)} %get-tuple-element.198, ...), kind=kOutput, calls=%fused_computation.69 | convolution fusion | flops 2451308544 | bytes 23246848 | tf_op jit(solution)/shard_map/lsd,de->lse/dot_general | solution.py:57
  114.7 14.8 %fusion.119 = (bf16[1536]{0:T(1024)(128)(2,1)}, bf16[8,256,1536]{2,1,0:T(8,128)(2,1)S(1)}) fusion(f32[8,256,1536]{2,1,0:T(8,128)} %get-tuple-element.210, f32[1536]{0:T(1024)} %reshape.154, bf16[1536,384]{1,0:T(8,128)(2,1)} %all-gather.9.cloned.1.call-done, bf16[8,256,384]{2,1,0:T(8,128)(2,1)} %param.29, f32[8,384]{1,0:T(8,128)} %get-tuple-element.196), kind=kOutput, calls=%fused_computation.174 | convolution fusion | flops 2487482880 | bytes 21648384 | tf_op jit(solution)/shard_map/lse,de->lsd/dot_general | solution.py:160
  129.5 3.6 fusion.92
  134.5 1.9 copy-done.37
  136.3 6.0 %fusion.79 = (bf16[8,384]{1,0:T(8,128)(2,1)}, bf16[8,256,384]{2,1,0:T(8,128)(2,1)}, bf16[8,384]{1,0:T(8,128)(2,1)}, f32[8,256]{1,0:T(8,128)S(1)}, f32[8,256]{1,0:T(8,128)S(1)}, /*index=5*/bf16[8,384]{1,0:T(8,128)(2,1)}) fusion(bf16[8,256,384]{2,1,0:T(8,128)(2,1)S(1)} %copy-done.9, f32[384]{0:T(512)S(1)} %copy-done.33, f32[8,256,384]{2,1,0:T(8,128)S(1)} %copy-done.2, ...), kind=kOutput, calls=%fused_computation.94 | convolution fusion | flops 2428488704 | bytes 16985600 | tf_op jit(solution)/shard_map/lsd,de->lse/dot_general | solution.py:57
  142.4 4.1 fusion.113
  146.5 2.3 convolution_convert_fusion.1
  148.7 3.1 fusion.85
  151.8 2.6 copy.82
  158.5 37.4 %while.27 = (s32[]{:T(128)}, bf16[4,2,256,6,64]{2,4,3,1,0:T(8,128)(2,1)}, bf16[4,2,256,6,64]{2,4,3,1,0:T(8,128)(2,1)}, bf16[4,2,256,6,64]{2,4,3,1,0:T(8,128)(2,1...) while((s32[]{:T(128)}, ...), condition=%wide.region_12.13_spmd, body=%wide.region_10.12_spmd.sunk | while | flops 513733632 | bytes 33916036 | solution.py:175
  158.5 1.7 fusion.161
  160.3 1.9 multiply_reduce_fusion.11
  164.3 2.1 fusion.162
  167.8 1.7 fusion.161
  169.6 1.9 multiply_reduce_fusion.11
  173.6 2.1 fusion.162
  177.2 1.7 fusion.161
  178.9 1.9 multiply_reduce_fusion.11
  182.9 2.1 fusion.162
  186.5 1.7 fusion.161
  188.3 1.9 multiply_reduce_fusion.11
  192.3 2.2 fusion.162
  195.9 2.8 copy.83
  200.2 2.7 copy.85
  203.1 5.3 %fusion.82 = bf16[384,1152]{1,0:T(8,128)(2,1)} fusion(bf16[8,256,384]{2,1,0:T(8,128)(2,1)S(1)} %copy-done, f32[8,384]{1,0:T(8,128)S(1)} %copy-done.20, f32[8,384]{1,0:T(8,128)S(1)} %get-tuple-element.200, f32[8,256]{1,0:T(8,128)S(1)} %add_rsqrt_fusion.1, f32[8,256]{1,0:T(8,128)S(1)} %broadcast_multiply_fusion.5, bf16[8,256,384]{2,1,0:T(8,128)(2,1)} %copy.85, ...), kind=kOutput, calls=%fused_computation.111 | convolution fusion | flops 1831256064 | bytes 7217152 | tf_op jit(solution)/shard_map/lsd,lse->de/dot_general | solution.py:61
  208.5 7.7 %fusion.83 = bf16[384,1536]{1,0:T(8,128)(2,1)} fusion(bf16[8,256,1536]{2,1,0:T(8,128)(2,1)} %copy-done.36, f32[8,256,384]{2,1,0:T(8,128)} %copy-done.1, f32[8,384]{1,0:T(8,128)S(1)} %copy-done.25, f32[8,384]{1,0:T(8,128)S(1)} %copy-done.18, f32[8,256]{1,0:T(8,128)S(1)} %copy-done.22, f32[8,256]{1,0:T(8,128)S(1)} %broadcast_multiply_fusion.4), kind=kOutput, calls=%fused_computation.112 | convolution fusion | flops 2420441088 | bytes 10657792 | tf_op jit(solution)/shard_map/lsd,lse->de/dot_general | solution.py:61
  216.2 11.4 %all_gather.43 = bf16[384,1152]{1,0:T(8,128)(2,1)} all-gather(bf16[96,1152]{1,0:T(8,128)(2,1)} %param.21), channel_id=1, replica_groups=mesh['rep'=8,'shard'=4] {'shard'}, dimensions={0}, use_global_device_ids=true | all-gather | bytes 1105920 | tf_op jit(solution)/shard_map/all_gather | solution.py:149
  227.6 7.7 %fusion.84 = bf16[1536,384]{1,0:T(8,128)(2,1)} fusion(bf16[8,256,1536]{2,1,0:T(8,128)(2,1)} %get-tuple-element.209, bf16[8,256,384]{2,1,0:T(8,128)(2,1)} %param.29, f32[8,384]{1,0:T(8,128)S(1)} %copy-done.16), kind=kOutput, calls=%fused_computation.113 | convolution fusion | flops 2418868224 | bytes 9056256 | tf_op jit(solution)/shard_map/lsd,lse->de/dot_general | solution.py:61
  235.5 6.2 %fusion.76 = (bf16[8,384]{1,0:T(8,128)(2,1)S(1)}, f32[8,256]{1,0:T(8,128)S(1)}, f32[8,256]{1,0:T(8,128)S(1)}, bf16[8,384]{1,0:T(8,128)(2,1)S(1)}, f32[8,256,384]{2,1,0:T(8,128)S(1)}) fusion(bf16[8,256,384]{2,1,0:T(8,128)(2,1)S(1)} %copy-done, f32[8,256]{1,0:T(8,128)S(1)} %add_rsqrt_fusion.1, f32[8,256]{1,0:T(8,128)S(1)} %broadcast_multiply_fusion.5, ...), kind=kOutput, calls=%fused_computation.91 | convolution fusion | flops 1833949184 | bytes 10379264 | tf_op jit(solution)/shard_map/lse,de->lsd/dot_general | solution.py:189
  241.8 3.1 multiply_reduce_fusion.3
  245.0 1.9 convolution_convert_fusion
  247.0 4.8 %reduce-scatter.8.cloned.1.call-done = bf16[96,1152]{1,0:T(8,128)(2,1)} async-done(((bf16[384,1152]{1,0:T(8,128)(2,1)}), bf16[96,1152]{1,0:T(8,128)(2,1)}) %reduce-scatter.8.cloned.1.call-update) | async-done | bytes 221200 | tf_op jit(solution)/shard_map/reduce_scatter | solution.py:207
  251.9 28.1 %reduce-scatter.12.cloned.1.call-done = bf16[96,1536]{1,0:T(8,128)(2,1)} async-done(((bf16[384,1536]{1,0:T(8,128)(2,1)}), bf16[96,1536]{1,0:T(8,128)(2,1)}) %reduce-scatter.12.cloned.1.call-update) | async-done | bytes 294928 | tf_op jit(solution)/shard_map/reduce_scatter | solution.py:219
  280.0 28.5 %reduce-scatter.14.cloned.1.call-done = bf16[384,384]{1,0:T(8,128)(2,1)} async-done(((bf16[1536,384]{1,0:T(8,128)(2,1)}), bf16[384,384]{1,0:T(8,128)(2,1)}) %reduce-scatter.14.cloned.1.call-update) | async-done | bytes 294928 | tf_op jit(solution)/shard_map/reduce_scatter | solution.py:225
  308.5 32.0 %reduce-scatter.6.cloned.1.call-done = bf16[96,2304]{1,0:T(8,128)(2,1)} async-done(((bf16[384,2304]{1,0:T(8,128)(2,1)}), bf16[96,2304]{1,0:T(8,128)(2,1)}) %reduce-scatter.6.cloned.1.call-update) | async-done | bytes 442384 | tf_op jit(solution)/shard_map/reduce_scatter | solution.py:201
  343.1 2.2 fusion.112
  345.4 10.5 %all-reduce.11 = (bf16[2304]{0:T(1024)(128)(2,1)S(1)}, bf16[768]{0:T(1024)(128)(2,1)S(1)}, bf16[384]{0:T(512)(128)(2,1)S(1)}, bf16[1536]{0:T(1024)(128)(2,1)S(1)}, bf16[384]{0:T(512)(128)(2,1)S(1)}) all-reduce(bf16[2304]{0:T(1024)(128)(2,1)S(1)} %reduce_sum.215, ...), channel_id=3, replica_groups=mesh['rep'=8,'shard'=4] {'shard'}, use_global_device_ids=true, to_apply=%region_24.25.clone | all-reduce | flops 5376 | bytes 21504
  356.4 22.2 %all-reduce.9 = (bf16[576]{0:T(1024)(128)(2,1)S(1)}, bf16[192]{0:T(256)(128)(2,1)S(1)}, bf16[96]{0:T(256)(128)(2,1)S(1)}, bf16[384]{0:T(512)(128)(2,1)S(1)}, bf16[96]{0:T(256)(128)(2,1)S(1)}) all-reduce(bf16[576]{0:T(1024)(128)(2,1)S(1)} %dynamic-slice.5, ...), channel_id=1, replica_groups=mesh['rep'=8,'shard'=4] {'rep'}, use_global_device_ids=true, to_apply=%region_25.26 | all-reduce | flops 1344 | bytes 5376 | tf_op jit(solution)/shard_map/psum | solution.py:234
  382.5 47.9 %all-reduce.15.cloned.1.call-done = (bf16[96,2304]{1,0:T(8,128)(2,1)}, bf16[96,1152]{1,0:T(8,128)(2,1)}, bf16[96,384]{1,0:T(8,128)(2,1)}, bf16[96,1536]{1,0:T(8,128)(2,1)}, bf16[384,384]{1,0:T(8,128)(2,1)}) async-done(((bf16[96,2304]{1,0:T(8,128)(2,1)}, bf16[96,1152]{1,0:T(8,128)(2,1)}, bf16[96,384]{1,0:T(8,128)(2,1)}, bf16[96,1536]{1,0:T(8,128)(2,1)}, bf16[384,384]{1,0:T(8,128)(2,1)}), ...) | async-done | bytes 1327120 | tf_op jit(solution)/shard_map/psum | solution.py:233
  430.4 2.0 convert_element_type.189
  432.5 1.8 convert_element_type.199
  434.3 1.8 convert_element_type.202
  (188 shorter events, 45.6 us)
Async XLA Ops:
  7.2 38.2 %copy-start.10 = (bf16[96,1152]{1,0:T(8,128)(2,1)S(1)}, bf16[96,1152]{1,0:T(8,128)(2,1)}, u32[]{:S(2)}) copy-start(bf16[96,1152]{1,0:T(8,128)(2,1)} %param.21) | copy-start | bytes 663556
  7.2 37.3 %copy-start = (bf16[8,256,384]{2,1,0:T(8,128)(2,1)S(1)}, bf16[8,256,384]{2,1,0:T(8,128)(2,1)}, u32[]{:S(2)}) copy-start(bf16[8,256,384]{2,1,0:T(8,128)(2,1)} %param.17) | copy-start | bytes 4718596
  7.2 53.4 %all-gather.5.cloned.1.call-start = ((), (), s32[]{:S(2)}) async-start(), calls=%async_computation.5 | async-start | bytes 2211840 | tf_op jit(solution)/shard_map/all_gather | solution.py:108
  7.9 95.7 %all-gather.7.cloned.1.call-start = ((), (), s32[]{:S(2)}) async-start(), calls=%async_computation.6 | async-start | bytes 1474560 | tf_op jit(solution)/shard_map/all_gather | solution.py:114
  8.7 106.0 %all-gather.9.cloned.1.call-start = ((), (), s32[]{:S(2)}) async-start(), calls=%async_computation.7 | async-start | bytes 1474560 | tf_op jit(solution)/shard_map/all_gather | solution.py:116
  8.7 36.7 %collective-permute-start = (bf16[1,96,1152]{2,1,0:T(8,128)(2,1)}, bf16[1,96,1152]{2,1,0:T(8,128)(2,1)S(1)}, u32[]{:S(2)}, u32[]{:S(2)}) collective-permute-start(bf16[1,96,1152]{2,1,0:T(8,128)(2,1)} %bitcast.183), channel_id=1, source_target_pairs={{0,1},{1,0},{2,3},{3,2},{4,5},{5,4},{6,7},{7,6},{8,9},{9,8},{10,11... | collective-permute-start | bytes 663560 | tf_op jit(solution)/shard_map/ppermute | solution.py:27
  9.4 237.6 %reduce-scatter.10.cloned.1.call-start = ((), (), s32[]{:S(2)}) async-start(), calls=%async_computation.10 | async-start | bytes 368640 | tf_op jit(solution)/shard_map/reduce_scatter | solution.py:213
  31.4 64.7 %copy-start.23 = (f32[384]{0:T(512)}, f32[384]{0:T(512)S(1)}, u32[]{:S(2)}) copy-start(f32[384]{0:T(512)S(1)} %convert_element_type.177) | copy-start | bytes 4612
  44.5 16.1 %copy-start.13 = (bf16[8,384]{1,0:T(8,128)(2,1)S(1)}, bf16[8,384]{1,0:T(8,128)(2,1)}, u32[]{:S(2)}) copy-start(bf16[8,384]{1,0:T(8,128)(2,1)} %param.18) | copy-start | bytes 18436
  45.5 14.9 %collective-permute-start.1 = (bf16[2,96,1152]{2,1,0:T(8,128)(2,1)S(1)}, bf16[2,96,1152]{2,1,0:T(8,128)(2,1)S(1)}, u32[]{:S(2)}, u32[]{:S(2)}) collective-permute-start(bf16[2,96,1152]{2,1,0:T(8,128)(2,1)S(1)} %pad_maximum_fusion.2), channel_id=1, source_target_pairs={{0,2},{1,3},{2,0},{3,1},{4,6},{5,7},{6,4},{7,5},{8,10},{9,11},{10,... | collective-permute-start | bytes 1327112 | tf_op jit(solution)/shard_map/ppermute | solution.py:27
  63.1 3.0 copy-start.19
  66.1 1.4 copy-start.26
  100.7 1.7 copy-start.1
  114.6 14.8 %copy-start.34 = (bf16[384,1536]{1,0:T(8,128)(2,1)S(1)}, bf16[384,1536]{1,0:T(8,128)(2,1)}, u32[]{:S(2)}) copy-start(bf16[384,1536]{1,0:T(8,128)(2,1)} %all-gather.7.cloned.1.call-done) | copy-start | bytes 3538948
  129.4 3.7 copy-start.36
  129.4 4.2 copy-start.2
  129.4 4.6 %copy-start.9 = (bf16[8,256,384]{2,1,0:T(8,128)(2,1)S(1)}, bf16[8,256,384]{2,1,0:T(8,128)(2,1)}, u32[]{:S(2)}) copy-start(bf16[8,256,384]{2,1,0:T(8,128)(2,1)} %param.29) | copy-start | bytes 4718596
  129.4 4.6 %copy-start.15 = (f32[8,384]{1,0:T(8,128)S(1)}, f32[8,384]{1,0:T(8,128)}, u32[]{:S(2)}) copy-start(f32[8,384]{1,0:T(8,128)} %get-tuple-element.196) | copy-start | bytes 36868
  129.5 4.6 %copy-start.17 = (f32[8,384]{1,0:T(8,128)S(1)}, f32[8,384]{1,0:T(8,128)}, u32[]{:S(2)}) copy-start(f32[8,384]{1,0:T(8,128)} %get-tuple-element.198) | copy-start | bytes 36868
  129.5 4.6 %copy-start.21 = (f32[8,256]{1,0:T(8,128)S(1)}, f32[8,256]{1,0:T(8,128)}, u32[]{:S(2)}) copy-start(f32[8,256]{1,0:T(8,128)} %add_rsqrt_fusion) | copy-start | bytes 24580
  129.5 4.6 %copy-start.33 = (f32[384]{0:T(512)S(1)}, f32[384]{0:T(512)}, u32[]{:S(2)}) copy-start(f32[384]{0:T(512)} %convert_element_type.181) | copy-start | bytes 4612
  129.5 5.0 %copy-start.35 = (bf16[1536,384]{1,0:T(8,128)(2,1)S(1)}, bf16[1536,384]{1,0:T(8,128)(2,1)}, u32[]{:S(2)}) copy-start(bf16[1536,384]{1,0:T(8,128)(2,1)} %all-gather.9.cloned.1.call-done) | copy-start | bytes 3538948
  129.5 6.8 %copy-start.37 = (bf16[8,256,1536]{2,1,0:T(8,128)(2,1)S(1)}, bf16[8,256,1536]{2,1,0:T(8,128)(2,1)}, u32[]{:S(2)}) copy-start(bf16[8,256,1536]{2,1,0:T(8,128)(2,1)} %get-tuple-element.209) | copy-start | bytes 18874372
  158.5 1.8 copy-start.3
  167.8 1.8 copy-start.3
  177.2 1.8 copy-start.3
  186.5 1.8 copy-start.3
  195.9 2.8 copy-start.7
  198.6 4.4 copy-start.20
  200.2 2.9 copy-start.8
  203.0 5.5 %copy-start.18 = (f32[8,384]{1,0:T(8,128)S(1)}, f32[8,384]{1,0:T(8,128)}, u32[]{:S(2)}) copy-start(f32[8,384]{1,0:T(8,128)} %get-tuple-element.198) | copy-start | bytes 36868
  203.0 5.5 %copy-start.22 = (f32[8,256]{1,0:T(8,128)S(1)}, f32[8,256]{1,0:T(8,128)}, u32[]{:S(2)}) copy-start(f32[8,256]{1,0:T(8,128)} %add_rsqrt_fusion) | copy-start | bytes 24580
  203.0 5.5 %copy-start.25 = (f32[8,384]{1,0:T(8,128)S(1)}, f32[8,384]{1,0:T(8,128)}, u32[]{:S(2)}) copy-start(f32[8,384]{1,0:T(8,128)} %get-tuple-element.197) | copy-start | bytes 36868
  203.0 48.9 %reduce-scatter.8.cloned.1.call-start = ((), (), s32[]{:S(2)}) async-start(), calls=%async_computation.9 | async-start | bytes 1105920 | tf_op jit(solution)/shard_map/reduce_scatter | solution.py:207
  208.4 19.3 %copy-start.16 = (f32[8,384]{1,0:T(8,128)S(1)}, f32[8,384]{1,0:T(8,128)}, u32[]{:S(2)}) copy-start(f32[8,384]{1,0:T(8,128)} %get-tuple-element.196) | copy-start | bytes 36868
  208.4 71.6 %reduce-scatter.12.cloned.1.call-start = ((), (), s32[]{:S(2)}) async-start(), calls=%async_computation.11 | async-start | bytes 1474560 | tf_op jit(solution)/shard_map/reduce_scatter | solution.py:219
  216.2 92.3 %reduce-scatter.14.cloned.1.call-start = ((), (), s32[]{:S(2)}) async-start(), calls=%async_computation.12 | async-start | bytes 1474560 | tf_op jit(solution)/shard_map/reduce_scatter | solution.py:225
  235.4 6.3 %copy-start.24 = (f32[384]{0:T(512)S(1)}, f32[384]{0:T(512)}, u32[]{:S(2)}) copy-start(f32[384]{0:T(512)} %copy-done.23) | copy-start | bytes 4612
  235.4 105.1 %reduce-scatter.6.cloned.1.call-start = ((), (), s32[]{:S(2)}) async-start(), calls=%async_computation.8 | async-start | bytes 2211840 | tf_op jit(solution)/shard_map/reduce_scatter | solution.py:201
  235.5 6.3 %copy-start.4 = (f32[8,256,384]{2,1,0:T(8,128)S(1)}, f32[8,256,384]{2,1,0:T(8,128)}, u32[]{:S(2)}) copy-start(f32[8,256,384]{2,1,0:T(8,128)} %get-tuple-element.208) | copy-start | bytes 9437188
  235.5 6.3 %copy-start.5 = (f32[8,256,384]{2,1,0:T(8,128)S(1)}, f32[8,256,384]{2,1,0:T(8,128)}, u32[]{:S(2)}) copy-start(f32[8,256,384]{2,1,0:T(8,128)} %get-tuple-element.174) | copy-start | bytes 9437188
  241.7 3.2 copy-start.29
  241.8 3.2 copy-start.28
  241.8 3.2 copy-start.27
  241.8 3.2 copy-start.14
  246.9 98.5 %copy-start.30 = (bf16[384]{0:T(512)(128)(2,1)S(1)}, bf16[384]{0:T(512)(128)(2,1)}, u32[]{:S(2)}) copy-start(bf16[384]{0:T(512)(128)(2,1)} %get-tuple-element.172) | copy-start | bytes 2308
  246.9 98.5 %copy-start.31 = (bf16[384]{0:T(512)(128)(2,1)S(1)}, bf16[384]{0:T(512)(128)(2,1)}, u32[]{:S(2)}) copy-start(bf16[384]{0:T(512)(128)(2,1)} %get-tuple-element.191) | copy-start | bytes 2308
  246.9 98.5 %copy-start.32 = (bf16[1536]{0:T(1024)(128)(2,1)S(1)}, bf16[1536]{0:T(1024)(128)(2,1)}, u32[]{:S(2)}) copy-start(bf16[1536]{0:T(1024)(128)(2,1)} %get-tuple-element.212) | copy-start | bytes 9220
  247.0 134.4 %copy-start.6 = (bf16[384,2304]{1,0:T(8,128)(2,1)S(1)}, bf16[384,2304]{1,0:T(8,128)(2,1)}, u32[]{:S(2)}) copy-start(bf16[384,2304]{1,0:T(8,128)(2,1)} %all-gather.5.cloned.1.call-done) | copy-start | bytes 5308420
  247.0 183.5 %all-reduce.15.cloned.1.call-start = ((), (), s32[]{:S(2)}) async-start(), calls=%async_computation.13 | async-start | bytes 2654208 | tf_op jit(solution)/shard_map/psum | solution.py:233
  430.4 5.7 %copy-start.11 = (bf16[96,1152]{1,0:T(8,128)(2,1)S(1)}, bf16[96,1152]{1,0:T(8,128)(2,1)}, u32[]{:S(2)}) copy-start(bf16[96,1152]{1,0:T(8,128)(2,1)} %get-tuple-element.159) | copy-start | bytes 663556
  430.4 6.5 %copy-start.12 = (bf16[96,384]{1,0:T(8,128)(2,1)S(1)}, bf16[96,384]{1,0:T(8,128)(2,1)}, u32[]{:S(2)}) copy-start(bf16[96,384]{1,0:T(8,128)(2,1)} %get-tuple-element.160) | copy-start | bytes 221188
Sparse Core Ops, SparseCore 0:
  9.6 23.6 all-gather.4
  34.9 19.9 all-gather.6
  56.4 17.1 all-gather.8
  203.1 21.7 reduce-scatter.9
  228.0 23.8 reduce-scatter.7
  254.3 25.6 reduce-scatter.11
  282.8 25.7 reduce-scatter.13
  311.1 29.3 reduce-scatter.5
  345.1 85.3 all-reduce.14
